TPU v7x, 256 devices: a whole 4x4x8 slice. The times are simulated.
256 devices in a mesh: row: 16 (over y_lo, z), vec: 16 (over y_hi, x, core).
Axes of the slice: x: 4, y: 4 (y_hi: 2, y_lo: 2; y = y_hi * 2 + y_lo), z: 8, core: 2. Of those that a mesh axis runs over, the one named last changes fastest.
Arguments:
- vectors: float32 [16384, 6144], P('row', 'vec'), may hold values from -6 to 6
- reflectors: float32 [64, 512, 256], P('row', 'vec'), may hold values from -0.25 to 0.25
- inner_factors: float32 [64, 256, 256], P('row', 'vec'), may hold values from -0.375 to 0.375
- offsets: int32 [2, 32], P(None, 'row'), may hold values from 0 to 15872, as said below
- owners: int32 [2, 32], P(None, 'row'), may hold values from 0 to 3, as said below
Outputs:
- result: float32 [16384, 6144], P('row', 'vec')
Inputs may be any that keep to these rules, and one draw needn't show every extreme that they name: `offsets`: within each sweep the columns j * 2 to (j + 1) * 2 - 1 belong to panel j, the rows j * 1024 to (j + 1) * 1024 - 1; a panel's start rows increase and are multiples of 256. A first-sweep block lies within its panel. A second-sweep block starts 256 rows or more after its panel's first row; in every panel but the last, the last second-sweep block starts at the panel's end minus 256, so it runs 256 rows into the next panel; the last panel's second-sweep blocks lie within it. `owners`: for each panel, its 4 entries (both sweeps) are a permutation of 0 to 3.
All inputs are finite; a program needn't handle non-finite values.
Results may differ from a plain program's by a relative error of at most 0.0001.
Values sent between devices are 32-bit elements; how exact they have to be, the bound alone decides.
No kernel may reach another device: no remote copies, remote signals or barrier semaphores. Data moves between devices by JAX's collectives and lax.ppermute only.
A program may use at most 64 MiB of HBM per device.

v0:
```python
import jax
import jax.numpy as jnp
from jax import lax
from jax.sharding import PartitionSpec as P


def from_behind(block, axis, distance):
    devices = range(lax.axis_size(axis))
    route = [(i - distance, i) for i in devices if i - distance in devices]
    return lax.ppermute(block, axis, route)


def contract_rows(left, right):
    return lax.dot_general(
        left,
        right,
        (((0,), (0,)), ((), ())),
        precision=lax.Precision.HIGHEST,
        preferred_element_type=jnp.float32,
    )


def multiply(left, right):
    return jnp.dot(left, right, precision=lax.Precision.HIGHEST, preferred_element_type=jnp.float32)


def shards(vectors, reflectors, inner_factors, offsets, owners):
    rows_dev = vectors.shape[0]
    reflect_count = reflectors.shape[2]
    block_rows = 2 * reflect_count
    per_sweep = offsets.shape[1]
    first_row = lax.axis_index("row") * rows_dev

    def fetch_block(owner_code):
        stored_basis = lax.dynamic_index_in_dim(reflectors, owner_code, 0, keepdims=False)
        stored_inner = lax.dynamic_index_in_dim(inner_factors, owner_code, 0, keepdims=False)
        return (
            lax.all_gather(stored_basis, "vec", axis=0, tiled=True),
            lax.all_gather(stored_inner, "vec", axis=0, tiled=True),
        )

    def run_sweep(current, sweep_index):

        def apply_block(block_index, current_rows):
            start_row = offsets[sweep_index, block_index] - first_row
            basis_block, inner_block = fetch_block(owners[sweep_index, block_index])
            window = lax.dynamic_slice_in_dim(current_rows, start_row, block_rows, 0)
            projection = contract_rows(basis_block, window)
            coupled = multiply(inner_block, projection)
            window = window - multiply(basis_block, coupled)
            return lax.dynamic_update_slice_in_dim(current_rows, window, start_row, 0)

        return lax.fori_loop(0, per_sweep, apply_block, current)

    after_first = run_sweep(vectors, 0)
    below_rows = from_behind(after_first[:reflect_count], "row", -1)
    extended = jnp.concatenate([after_first, below_rows], 0)
    extended = run_sweep(extended, 1)
    handed = from_behind(extended[rows_dev:], "row", 1)
    head_rows = jnp.where(lax.axis_index("row") > 0, handed, extended[:reflect_count])
    return jnp.concatenate([head_rows, extended[reflect_count:rows_dev]], 0)


def solution(mesh):
    return jax.shard_map(
        shards,
        mesh=mesh,
        in_specs=(
            P("row", "vec"),
            P("row", "vec", None),
            P("row", "vec", None),
            P(None, "row"),
            P(None, "row"),
        ),
        out_specs=P("row", "vec"),
        check_vma=False,
    )
```

profile of v0, /device:TPU:10, one launch (start us, length us, event | category | flops | bytes accessed | tf_op | source)
XLA Modules:
  0.0 253.6 jit_solution(5335601532820274075)
XLA Ops:
  0.0 1.4 copy-done
  1.4 109.5 %while.26 = (s32[]{:T(128)}, f32[1024,384]{1,0:T(8,128)S(1)}, s32[2,2]{1,0:T(2,128)S(1)}, s32[]{:T(128)}, s32[2,2]{1,0:T(2,128)S(1)}, /*index=5*/f32[4,32,256]{2...) while((s32[]{:T(128)}, f32[1024,384]{1,0:T(8,128)S(1)}, ...), condition=%wide.region_1.2_spmd, body=%wide.region_0.1_spmd.sunk | while | flops 1510146048 | bytes 7749873 | solution.py:53
  7.0 20.2 %all-gather.9 = f32[1,256,256]{2,1,0:T(8,128)S(1)} all-gather(f32[1,16,256]{2,1,0:T(8,128)S(1)} %constant_dynamic-slice_fusion.19), channel_id=3, replica_groups=mesh['row'=16,'vec'=16] {'vec'}, dimensions={1}, use_global_device_ids=true | all-gather | bytes 278528 | tf_op jit(solution)/shard_map/while/body/eval_jaxpr/all_gather | solution.py:39
  27.2 24.8 %all-gather.8 = f32[1,512,256]{2,1,0:T(8,128)S(1)} all-gather(f32[1,32,256]{2,1,0:T(8,128)S(1)} %constant_dynamic-slice_fusion.18), channel_id=2, replica_groups=mesh['row'=16,'vec'=16] {'vec'}, dimensions={1}, use_global_device_ids=true | all-gather | bytes 557056 | tf_op jit(solution)/shard_map/while/body/eval_jaxpr/all_gather | solution.py:38
  52.0 1.1 fusion.40
  54.7 3.0 %dynamic_update_slice.16 = f32[1024,384]{1,0:T(8,128)S(1)} dynamic-update-slice(f32[1024,384]{1,0:T(8,128)S(1)} %get-tuple-element.381, f32[512,384]{1,0:T(8,128)S(1)} %convolution_subtract_fusion.4, s32[]{:T(128)S(6)} %select_n.62, s32[]{:T(128)} %constant.85.clone.1..sunk) | dynamic-update-slice | bytes 1572868 | tf_op jit(solution)/shard_map/while/body/eval_jaxpr/dynamic_update_slice | solution.py:51
  63.3 20.0 %all-gather.9 = f32[1,256,256]{2,1,0:T(8,128)S(1)} all-gather(f32[1,16,256]{2,1,0:T(8,128)S(1)} %constant_dynamic-slice_fusion.19), channel_id=3, replica_groups=mesh['row'=16,'vec'=16] {'vec'}, dimensions={1}, use_global_device_ids=true | all-gather | bytes 278528 | tf_op jit(solution)/shard_map/while/body/eval_jaxpr/all_gather | solution.py:39
  83.3 22.0 %all-gather.8 = f32[1,512,256]{2,1,0:T(8,128)S(1)} all-gather(f32[1,32,256]{2,1,0:T(8,128)S(1)} %constant_dynamic-slice_fusion.18), channel_id=2, replica_groups=mesh['row'=16,'vec'=16] {'vec'}, dimensions={1}, use_global_device_ids=true | all-gather | bytes 557056 | tf_op jit(solution)/shard_map/while/body/eval_jaxpr/all_gather | solution.py:38
  105.3 1.1 fusion.40
  108.0 2.9 %dynamic_update_slice.16 = f32[1024,384]{1,0:T(8,128)S(1)} dynamic-update-slice(f32[1024,384]{1,0:T(8,128)S(1)} %get-tuple-element.381, f32[512,384]{1,0:T(8,128)S(1)} %convolution_subtract_fusion.4, s32[]{:T(128)S(6)} %select_n.62, s32[]{:T(128)} %constant.85.clone.1..sunk) | dynamic-update-slice | bytes 1572868 | tf_op jit(solution)/shard_map/while/body/eval_jaxpr/dynamic_update_slice | solution.py:51
  110.9 8.5 %collective-permute-start = (f32[256,384]{1,0:T(8,128)S(1)}, f32[256,384]{1,0:T(8,128)}, u32[]{:S(2)}, u32[]{:S(2)}) collective-permute-start(f32[256,384]{1,0:T(8,128)S(1)} %slice.12), channel_id=1, source_target_pairs={{16,0},{32,16},{48,32},{64,48},{80,64},{96,80},{112,96},{128,112},... | collective-permute-start | bytes 1179656 | tf_op jit(solution)/shard_map/ppermute | solution.py:10
  119.5 8.9 %collective-permute-done = f32[256,384]{1,0:T(8,128)} collective-permute-done((f32[256,384]{1,0:T(8,128)S(1)}, f32[256,384]{1,0:T(8,128)}, u32[]{:S(2)}, u32[]{:S(2)}) %collective-permute-start) | collective-permute-done | bytes 393248 | tf_op jit(solution)/shard_map/ppermute | solution.py:10
  128.4 1.1 pad_maximum_fusion
  129.5 106.5 %while.27 = (s32[]{:T(128)}, f32[1280,384]{1,0:T(8,128)S(1)}, s32[2,2]{1,0:T(2,128)S(1)}, s32[]{:T(128)}, s32[2,2]{1,0:T(2,128)S(1)}, /*index=5*/f32[4,32,256]{2...) while((s32[]{:T(128)}, f32[1280,384]{1,0:T(8,128)S(1)}, ...), condition=%wide.region_3.4_spmd, body=%wide.region_2.3_spmd.sunk | while | flops 1510146048 | bytes 7749873 | solution.py:53
  135.1 20.0 %all-gather.11 = f32[1,256,256]{2,1,0:T(8,128)S(1)} all-gather(f32[1,16,256]{2,1,0:T(8,128)S(1)} %constant_dynamic-slice_fusion.23), channel_id=5, replica_groups=mesh['row'=16,'vec'=16] {'vec'}, dimensions={1}, use_global_device_ids=true | all-gather | bytes 278528 | tf_op jit(solution)/shard_map/while/body/eval_jaxpr/all_gather | solution.py:39
  155.1 22.0 %all-gather.10 = f32[1,512,256]{2,1,0:T(8,128)S(1)} all-gather(f32[1,32,256]{2,1,0:T(8,128)S(1)} %constant_dynamic-slice_fusion.22), channel_id=4, replica_groups=mesh['row'=16,'vec'=16] {'vec'}, dimensions={1}, use_global_device_ids=true | all-gather | bytes 557056 | tf_op jit(solution)/shard_map/while/body/eval_jaxpr/all_gather | solution.py:38
  179.8 3.0 %dynamic_update_slice.17 = f32[1280,384]{1,0:T(8,128)S(1)} dynamic-update-slice(f32[1280,384]{1,0:T(8,128)S(1)} %get-tuple-element.414, f32[512,384]{1,0:T(8,128)S(1)} %convolution_subtract_fusion.5, s32[]{:T(128)S(6)} %select_n.64, s32[]{:T(128)} %constant.85.clone.1..sunk.1) | dynamic-update-slice | bytes 1572868 | tf_op jit(solution)/shard_map/while/body/eval_jaxpr/dynamic_update_slice | solution.py:51
  188.4 20.0 %all-gather.11 = f32[1,256,256]{2,1,0:T(8,128)S(1)} all-gather(f32[1,16,256]{2,1,0:T(8,128)S(1)} %constant_dynamic-slice_fusion.23), channel_id=5, replica_groups=mesh['row'=16,'vec'=16] {'vec'}, dimensions={1}, use_global_device_ids=true | all-gather | bytes 278528 | tf_op jit(solution)/shard_map/while/body/eval_jaxpr/all_gather | solution.py:39
  208.3 22.0 %all-gather.10 = f32[1,512,256]{2,1,0:T(8,128)S(1)} all-gather(f32[1,32,256]{2,1,0:T(8,128)S(1)} %constant_dynamic-slice_fusion.22), channel_id=4, replica_groups=mesh['row'=16,'vec'=16] {'vec'}, dimensions={1}, use_global_device_ids=true | all-gather | bytes 557056 | tf_op jit(solution)/shard_map/while/body/eval_jaxpr/all_gather | solution.py:38
  230.4 1.1 fusion.48
  233.0 2.9 %dynamic_update_slice.17 = f32[1280,384]{1,0:T(8,128)S(1)} dynamic-update-slice(f32[1280,384]{1,0:T(8,128)S(1)} %get-tuple-element.414, f32[512,384]{1,0:T(8,128)S(1)} %convolution_subtract_fusion.5, s32[]{:T(128)S(6)} %select_n.64, s32[]{:T(128)} %constant.85.clone.1..sunk.1) | dynamic-update-slice | bytes 1572868 | tf_op jit(solution)/shard_map/while/body/eval_jaxpr/dynamic_update_slice | solution.py:51
  236.0 1.9 collective-permute-start.1
  238.1 14.2 %collective-permute-done.1 = f32[256,384]{1,0:T(8,128)S(1)} collective-permute-done((f32[256,384]{1,0:T(8,128)S(1)}, f32[256,384]{1,0:T(8,128)S(1)}, u32[]{:S(2)}, u32[]{:S(2)}) %collective-permute-start.1) | collective-permute-done | bytes 393248 | tf_op jit(solution)/shard_map/ppermute | solution.py:10
  252.3 1.2 pad_maximum_fusion.1
  (34 shorter events, 18.9 us)
Async XLA Ops:
  0.0 1.4 copy-start
  0.0 1.4 copy-start.1
  0.0 1.4 copy-start.2
  110.9 17.4 %collective-permute-start = (f32[256,384]{1,0:T(8,128)S(1)}, f32[256,384]{1,0:T(8,128)}, u32[]{:S(2)}, u32[]{:S(2)}) collective-permute-start(f32[256,384]{1,0:T(8,128)S(1)} %slice.12), channel_id=1, source_target_pairs={{16,0},{32,16},{48,32},{64,48},{80,64},{96,80},{112,96},{128,112},... | collective-permute-start | bytes 1179656 | tf_op jit(solution)/shard_map/ppermute | solution.py:10
  236.0 16.2 %collective-permute-start.1 = (f32[256,384]{1,0:T(8,128)S(1)}, f32[256,384]{1,0:T(8,128)S(1)}, u32[]{:S(2)}, u32[]{:S(2)}) collective-permute-start(f32[256,384]{1,0:T(8,128)S(1)} %slice.13), channel_id=1, source_target_pairs={{0,16},{16,32},{32,48},{48,64},{64,80},{80,96},{96,112},{112,128},... | collective-permute-start | bytes 1179656 | tf_op jit(solution)/shard_map/ppermute | solution.py:10
where the time goes:
time: 254 us
  blocking collectives  171 us (67%)
  local copies, waits for them, and re-layouts  24.7 us (10%)
  waiting for transfers between devices  23.1 us (9%)
  loops' own time  11.3 us (4%)
  matrix products  10.6 us (4%)
  starting transfers between devices  10.5 us (4%)
    all_gather x4, blocking collectives, fetch_block(): lax.all_gather(stored_basis, 'vec', axis=0, tiled=True)  90.9 us
    all_gather x4, blocking collectives, fetch_block(): lax.all_gather(stored_inner, 'vec', axis=0, tiled=True)  80 us
    ppermute x2, waiting for transfers between devices, from_behind(): return lax.ppermute(block, axis, route)  23.1 us
    dynamic_update_slice x4, local copies, waits for them, and re-layouts, apply_block(): return lax.dynamic_update_slice_in_dim(current_rows, window, start_row, 0)  11.9 us
    another operation x2, loops' own time, run_sweep(): return lax.fori_loop(0, per_sweep, apply_block, current)  11.3 us
    ppermute x2, starting transfers between devices, from_behind(): return lax.ppermute(block, axis, route)  10.5 us
    dot_general x8, matrix products, multiply(): jnp.dot(left, right, precision=lax.Precision.HIGHEST, preferred_element_t...  6.36 us
  transfers between devices with their start and end apart: 2, of which 2 were waited for; matrix products, arithmetic and copies ran while one was open for 0% of the time, Pallas kernels for 0%

commit v1 on v0

--- a/solution.py
+++ b/solution.py
@@ -1,7 +1,17 @@
+import functools
 import jax
 import jax.numpy as jnp
 from jax import lax
 from jax.sharding import PartitionSpec as P
+
+
+def quotas_start(a0, shard_axis, axis_k):
+    return jnp.concatenate(
+        lax.all_to_all(jnp.stack([a0] * lax.axis_size(shard_axis)), shard_axis, 0, 0), axis=axis_k
+    )
+
+
+local_data_try_all = functools.partial(quotas_start, shard_axis="vec", axis_k=0)
 
 
 def from_behind(block, axis, distance):
@@ -35,7 +45,7 @@
         stored_basis = lax.dynamic_index_in_dim(reflectors, owner_code, 0, keepdims=False)
         stored_inner = lax.dynamic_index_in_dim(inner_factors, owner_code, 0, keepdims=False)
         return (
-            lax.all_gather(stored_basis, "vec", axis=0, tiled=True),
+            local_data_try_all(stored_basis),
             lax.all_gather(stored_inner, "vec", axis=0, tiled=True),
         )
 

time: 254 us -> 202 us (0.80)
  blocking collectives: 171 us -> 92.7 us
  starting transfers between devices: 10.5 us -> 33.6 us
    all_gather x4 -> x0, blocking collectives: 90.9 us -> none  [fetch_block(): lax.all_gather(stored_basis, 'vec', axis=0, tiled=True)]
    all_to_all x0 -> x4, starting transfers between devices: none -> 23.2 us  [quotas_start(): lax.all_to_all(jnp.stack([a0] * lax.axis_size(shard_axis)), shard_axis, 0...]
    all_gather x4, blocking collectives: 80 us -> 92.7 us  [fetch_block(): lax.all_gather(stored_inner, 'vec', axis=0, tiled=True)]
    another operation x0 -> x4, local copies, waits for them, and re-layouts: none -> 3.38 us  [quotas_start(): jnp.stack([a0] * lax.axis_size(shard_axis))]
    dynamic_slice x4, local copies, waits for them, and re-layouts: 3.04 us -> 0.04 us  [fetch_block(): lax.dynamic_index_in_dim(reflectors, owner_code, 0, keepdims=False)]
    dynamic_slice x4, local copies, waits for them, and re-layouts: 2.89 us -> 0.04 us  [fetch_block(): lax.dynamic_index_in_dim(inner_factors, owner_code, 0, keepdims=False)]
    while x0 -> x8, local copies, waits for them, and re-layouts: none -> 2.62 us
  transfers between devices with their start and end apart: 2 -> 6, of which waited for: 2 -> 2; matrix products, arithmetic and copies ran while one was open for 0% -> 2% of each run, Pallas kernels for 0% -> 0%
where the time goes in v1:
time: 202 us; the launch traced here: 200 us
  blocking collectives  92.7 us (46%)
  starting transfers between devices  33.6 us (17%)
  local copies, waits for them, and re-layouts  26.7 us (13%)
  waiting for transfers between devices  21.7 us (11%)
  loops' own time  10.6 us (5%)
  matrix products  10.6 us (5%)
  other arithmetic  3.73 us (2%)
    all_gather x4, blocking collectives, fetch_block(): lax.all_gather(stored_inner, 'vec', axis=0, tiled=True)  92.7 us
    all_to_all x4, starting transfers between devices, quotas_start(): lax.all_to_all(jnp.stack([a0] * lax.axis_size(shard_axis)), shard_axis, 0...  23.2 us
    ppermute x2, waiting for transfers between devices, from_behind(): return lax.ppermute(block, axis, route)  21.7 us
    dynamic_update_slice x4, local copies, waits for them, and re-layouts, apply_block(): return lax.dynamic_update_slice_in_dim(current_rows, window, start_row, 0)  11.9 us
    another operation x2, loops' own time, run_sweep(): return lax.fori_loop(0, per_sweep, apply_block, current)  10.6 us
    ppermute x2, starting transfers between devices, from_behind(): return lax.ppermute(block, axis, route)  10.5 us
    dot_general x8, matrix products, multiply(): jnp.dot(left, right, precision=lax.Precision.HIGHEST, preferred_element_t...  6.35 us
    dot_general x4, matrix products, contract_rows(): lax.dot_general(left, right, (((0,), (0,)), ((), ())), precision=lax.Prec...  4.26 us
  transfers between devices with their start and end apart: 6, of which 2 were waited for; matrix products, arithmetic and copies ran while one was open for 2% of the time, Pallas kernels for 0%

profile of v1, /device:TPU:10, one launch (start us, length us, event | category | flops | bytes accessed | tf_op | source)
XLA Modules:
  0.0 199.8 jit_solution(16573110879465513029)
XLA Ops:
  0.0 1.4 copy-done
  1.4 79.2 %while.26 = (s32[]{:T(128)}, f32[1024,384]{1,0:T(8,128)S(1)}, s32[2,2]{1,0:T(2,128)S(1)}, s32[]{:T(128)}, s32[2,2]{1,0:T(2,128)S(1)}, /*index=5*/f32[4,32,256]{2...) while((s32[]{:T(128)}, f32[1024,384]{1,0:T(8,128)S(1)}, ...), condition=%wide.region_1.2_spmd, body=%wide.region_0.1_spmd.sunk | while | flops 1510146048 | bytes 9322769 | solution.py:63
  4.8 6.6 %all-to-all-start = ((f32[16,32,256]{2,1,0:T(8,128)}), f32[16,32,256]{2,1,0:T(8,128)S(1)}, u32[]{:S(2)}, u32[]{:S(2)}) async-start(f32[16,32,256]{2,1,0:T(8,128)} %stack.10), calls=%async_computation | async-start | bytes 1048576 | tf_op jit(solution)/shard_map/while/body/eval_jaxpr/all_to_all | solution.py:10
  12.7 23.1 %all-gather.4 = f32[1,256,256]{2,1,0:T(8,128)S(1)} all-gather(f32[1,16,256]{2,1,0:T(8,128)S(1)} %constant_dynamic-slice_fusion.14), channel_id=2, replica_groups=mesh['row'=16,'vec'=16] {'vec'}, dimensions={1}, use_global_device_ids=true | all-gather | bytes 278528 | tf_op jit(solution)/shard_map/while/body/eval_jaxpr/all_gather | solution.py:49
  38.5 3.0 %dynamic_update_slice.16 = f32[1024,384]{1,0:T(8,128)S(1)} dynamic-update-slice(f32[1024,384]{1,0:T(8,128)S(1)} %get-tuple-element.381, f32[512,384]{1,0:T(8,128)S(1)} %convolution_subtract_fusion.4, s32[]{:T(128)S(6)} %select_n.63, s32[]{:T(128)} %constant.85.clone.1..sunk) | dynamic-update-slice | bytes 1572868 | tf_op jit(solution)/shard_map/while/body/eval_jaxpr/dynamic_update_slice | solution.py:61
  44.9 5.5 %all-to-all-start = ((f32[16,32,256]{2,1,0:T(8,128)}), f32[16,32,256]{2,1,0:T(8,128)S(1)}, u32[]{:S(2)}, u32[]{:S(2)}) async-start(f32[16,32,256]{2,1,0:T(8,128)} %stack.10), calls=%async_computation | async-start | bytes 1048576 | tf_op jit(solution)/shard_map/while/body/eval_jaxpr/all_to_all | solution.py:10
  51.7 23.2 %all-gather.4 = f32[1,256,256]{2,1,0:T(8,128)S(1)} all-gather(f32[1,16,256]{2,1,0:T(8,128)S(1)} %constant_dynamic-slice_fusion.14), channel_id=2, replica_groups=mesh['row'=16,'vec'=16] {'vec'}, dimensions={1}, use_global_device_ids=true | all-gather | bytes 278528 | tf_op jit(solution)/shard_map/while/body/eval_jaxpr/all_gather | solution.py:49
  77.6 2.9 %dynamic_update_slice.16 = f32[1024,384]{1,0:T(8,128)S(1)} dynamic-update-slice(f32[1024,384]{1,0:T(8,128)S(1)} %get-tuple-element.381, f32[512,384]{1,0:T(8,128)S(1)} %convolution_subtract_fusion.4, s32[]{:T(128)S(6)} %select_n.63, s32[]{:T(128)} %constant.85.clone.1..sunk) | dynamic-update-slice | bytes 1572868 | tf_op jit(solution)/shard_map/while/body/eval_jaxpr/dynamic_update_slice | solution.py:61
  80.6 8.6 %collective-permute-start = (f32[256,384]{1,0:T(8,128)S(1)}, f32[256,384]{1,0:T(8,128)S(1)}, u32[]{:S(2)}, u32[]{:S(2)}) collective-permute-start(f32[256,384]{1,0:T(8,128)S(1)} %slice.12), channel_id=1, source_target_pairs={{16,0},{32,16},{48,32},{64,48},{80,64},{96,80},{112,96},{128,112},... | collective-permute-start | bytes 1179656 | tf_op jit(solution)/shard_map/ppermute | solution.py:20
  89.2 8.9 %collective-permute-done = f32[256,384]{1,0:T(8,128)S(1)} collective-permute-done((f32[256,384]{1,0:T(8,128)S(1)}, f32[256,384]{1,0:T(8,128)S(1)}, u32[]{:S(2)}, u32[]{:S(2)}) %collective-permute-start) | collective-permute-done | bytes 393248 | tf_op jit(solution)/shard_map/ppermute | solution.py:20
  98.0 1.4 pad_maximum_fusion
  99.5 80.9 %while.27 = (s32[]{:T(128)}, f32[1280,384]{1,0:T(8,128)}, s32[2,2]{1,0:T(2,128)S(1)}, s32[]{:T(128)}, s32[2,2]{1,0:T(2,128)S(1)}, /*index=5*/f32[4,32,256]{2,1,0...) while((s32[]{:T(128)}, f32[1280,384]{1,0:T(8,128)}, ...), condition=%wide.region_3.4_spmd, body=%wide.region_2.3_spmd.sunk | while | flops 1510146048 | bytes 25051464 | solution.py:63
  102.9 5.5 %all-to-all-start.1 = ((f32[16,32,256]{2,1,0:T(8,128)}), f32[16,32,256]{2,1,0:T(8,128)S(1)}, u32[]{:S(2)}, u32[]{:S(2)}) async-start(f32[16,32,256]{2,1,0:T(8,128)} %stack.11), calls=%async_computation.1 | async-start | bytes 1048576 | tf_op jit(solution)/shard_map/while/body/eval_jaxpr/all_to_all | solution.py:10
  109.7 23.2 %all-gather.5 = f32[1,256,256]{2,1,0:T(8,128)S(1)} all-gather(f32[1,16,256]{2,1,0:T(8,128)S(1)} %constant_dynamic-slice_fusion.17), channel_id=3, replica_groups=mesh['row'=16,'vec'=16] {'vec'}, dimensions={1}, use_global_device_ids=true | all-gather | bytes 278528 | tf_op jit(solution)/shard_map/while/body/eval_jaxpr/all_gather | solution.py:49
  135.6 3.0 %dynamic_update_slice.17 = f32[1280,384]{1,0:T(8,128)S(1)} dynamic-update-slice(f32[1280,384]{1,0:T(8,128)S(1)} %copy-done.1, f32[512,384]{1,0:T(8,128)S(1)} %convolution_subtract_fusion.5, s32[]{:T(128)S(6)} %select_n.65, s32[]{:T(128)} %constant.85.clone.1..sunk.1) | dynamic-update-slice | bytes 1572868 | tf_op jit(solution)/shard_map/while/body/eval_jaxpr/dynamic_update_slice | solution.py:61
  138.6 1.3 copy-done.2
  143.4 5.5 %all-to-all-start.1 = ((f32[16,32,256]{2,1,0:T(8,128)}), f32[16,32,256]{2,1,0:T(8,128)S(1)}, u32[]{:S(2)}, u32[]{:S(2)}) async-start(f32[16,32,256]{2,1,0:T(8,128)} %stack.11), calls=%async_computation.1 | async-start | bytes 1048576 | tf_op jit(solution)/shard_map/while/body/eval_jaxpr/all_to_all | solution.py:10
  150.2 23.2 %all-gather.5 = f32[1,256,256]{2,1,0:T(8,128)S(1)} all-gather(f32[1,16,256]{2,1,0:T(8,128)S(1)} %constant_dynamic-slice_fusion.17), channel_id=3, replica_groups=mesh['row'=16,'vec'=16] {'vec'}, dimensions={1}, use_global_device_ids=true | all-gather | bytes 278528 | tf_op jit(solution)/shard_map/while/body/eval_jaxpr/all_gather | solution.py:49
  176.1 2.9 %dynamic_update_slice.17 = f32[1280,384]{1,0:T(8,128)S(1)} dynamic-update-slice(f32[1280,384]{1,0:T(8,128)S(1)} %copy-done.1, f32[512,384]{1,0:T(8,128)S(1)} %convolution_subtract_fusion.5, s32[]{:T(128)S(6)} %select_n.65, s32[]{:T(128)} %constant.85.clone.1..sunk.1) | dynamic-update-slice | bytes 1572868 | tf_op jit(solution)/shard_map/while/body/eval_jaxpr/dynamic_update_slice | solution.py:61
  179.0 1.3 copy-done.2
  181.4 1.9 collective-permute-start.1
  183.3 1.3 slice.15
  184.6 12.8 %collective-permute-done.1 = f32[256,384]{1,0:T(8,128)S(1)} collective-permute-done((f32[256,384]{1,0:T(8,128)S(1)}, f32[256,384]{1,0:T(8,128)S(1)}, u32[]{:S(2)}, u32[]{:S(2)}) %collective-permute-start.1) | collective-permute-done | bytes 393248 | tf_op jit(solution)/shard_map/ppermute | solution.py:20
  198.5 1.2 pad_maximum_fusion.1
  (54 shorter events, 21.1 us)
Async XLA Ops:
  0.0 1.4 copy-start
  0.0 1.4 copy-start.3
  0.0 1.4 copy-start.4
  0.0 1.4 copy-start.5
  0.0 1.4 copy-start.6
  4.8 31.0 %all-to-all-start = ((f32[16,32,256]{2,1,0:T(8,128)}), f32[16,32,256]{2,1,0:T(8,128)S(1)}, u32[]{:S(2)}, u32[]{:S(2)}) async-start(f32[16,32,256]{2,1,0:T(8,128)} %stack.10), calls=%async_computation | async-start | bytes 1048576 | tf_op jit(solution)/shard_map/while/body/eval_jaxpr/all_to_all | solution.py:10
  44.9 30.0 %all-to-all-start = ((f32[16,32,256]{2,1,0:T(8,128)}), f32[16,32,256]{2,1,0:T(8,128)S(1)}, u32[]{:S(2)}, u32[]{:S(2)}) async-start(f32[16,32,256]{2,1,0:T(8,128)} %stack.10), calls=%async_computation | async-start | bytes 1048576 | tf_op jit(solution)/shard_map/while/body/eval_jaxpr/all_to_all | solution.py:10
  80.6 17.4 %collective-permute-start = (f32[256,384]{1,0:T(8,128)S(1)}, f32[256,384]{1,0:T(8,128)S(1)}, u32[]{:S(2)}, u32[]{:S(2)}) collective-permute-start(f32[256,384]{1,0:T(8,128)S(1)} %slice.12), channel_id=1, source_target_pairs={{16,0},{32,16},{48,32},{64,48},{80,64},{96,80},{112,96},{128,112},... | collective-permute-start | bytes 1179656 | tf_op jit(solution)/shard_map/ppermute | solution.py:20
  99.5 33.4 %copy-start.1 = (f32[1280,384]{1,0:T(8,128)S(1)}, f32[1280,384]{1,0:T(8,128)}, u32[]{:S(2)}) copy-start(f32[1280,384]{1,0:T(8,128)} %get-tuple-element.414) | copy-start | bytes 5898244 | tf_op jit(solution)/shard_map/while
  102.9 30.0 %all-to-all-start.1 = ((f32[16,32,256]{2,1,0:T(8,128)}), f32[16,32,256]{2,1,0:T(8,128)S(1)}, u32[]{:S(2)}, u32[]{:S(2)}) async-start(f32[16,32,256]{2,1,0:T(8,128)} %stack.11), calls=%async_computation.1 | async-start | bytes 1048576 | tf_op jit(solution)/shard_map/while/body/eval_jaxpr/all_to_all | solution.py:10
  138.6 1.3 copy-start.2
  139.9 33.5 %copy-start.1 = (f32[1280,384]{1,0:T(8,128)S(1)}, f32[1280,384]{1,0:T(8,128)}, u32[]{:S(2)}) copy-start(f32[1280,384]{1,0:T(8,128)} %get-tuple-element.414) | copy-start | bytes 5898244 | tf_op jit(solution)/shard_map/while
  143.4 30.0 %all-to-all-start.1 = ((f32[16,32,256]{2,1,0:T(8,128)}), f32[16,32,256]{2,1,0:T(8,128)S(1)}, u32[]{:S(2)}, u32[]{:S(2)}) async-start(f32[16,32,256]{2,1,0:T(8,128)} %stack.11), calls=%async_computation.1 | async-start | bytes 1048576 | tf_op jit(solution)/shard_map/while/body/eval_jaxpr/all_to_all | solution.py:10
  179.0 1.3 copy-start.2
  181.4 16.1 %collective-permute-start.1 = (f32[256,384]{1,0:T(8,128)S(1)}, f32[256,384]{1,0:T(8,128)S(1)}, u32[]{:S(2)}, u32[]{:S(2)}) collective-permute-start(f32[256,384]{1,0:T(8,128)S(1)} %slice.13), channel_id=1, source_target_pairs={{0,16},{16,32},{32,48},{48,64},{64,80},{80,96},{96,112},{112,128},... | collective-permute-start | bytes 1179656 | tf_op jit(solution)/shard_map/ppermute | solution.py:20
